TPU v7x, 32 devices: a whole 2x2x4 slice. The times are simulated.
32 devices in a mesh: groups: 2 (over x), expert: 16 (over z, y, core).
Axes of the slice: x: 2, y: 2, z: 4, core: 2. Of those that a mesh axis runs over, the one named last changes fastest.
Arguments:
- tokens: bfloat16 [4096, 2048], P(('groups', 'expert')), parts along dimension 0, may hold values from -6 to 6
- out_grad: bfloat16 [4096, 2048], P(('groups', 'expert')), parts along dimension 0, may hold values from -6 to 6
- gate_probs: float32 [4096, 8], P(('groups', 'expert')), parts along dimension 0, may hold values from 0.05 to 0.2
- routes: int32 [4096, 8], P(('groups', 'expert')), parts along dimension 0, may hold values from 0 to 15, all different within a row; in each aligned block of 128 rows (0 to 127, 128 to 255, ...) at most 80 rows name the same one
- w_gate: bfloat16 [16, 2048, 384], P('expert'), may hold values from -0.125 to 0.125
- w_up: bfloat16 [16, 2048, 384], P('expert'), may hold values from -0.125 to 0.125
- w_down: bfloat16 [16, 384, 2048], P('expert'), may hold values from -0.3125 to 0.3125
Outputs:
- tokens_grad: bfloat16 [4096, 2048], P(('groups', 'expert')), parts along dimension 0
- gate_wgrad: bfloat16 [32, 2048, 384], P(('groups', 'expert')), parts along dimension 0
- up_wgrad: bfloat16 [32, 2048, 384], P(('groups', 'expert')), parts along dimension 0
- down_wgrad: bfloat16 [32, 384, 2048], P(('groups', 'expert')), parts along dimension 0
There are 2 independent parts, one for each index of `groups`. A program takes and returns all parts, laid end to end along the dimension named above; an argument that names none is the same for every part. Nothing has to cross between parts.
Inputs may be any that keep to these rules, and one draw needn't show every extreme that they name: A token's 8 experts differ. Among the 128 tokens of one block no expert is named by more than 80 routes, and in some block one expert is named by exactly 80.
All inputs are finite; a program needn't handle non-finite values.
Results may differ from a plain program's by a relative error of at most 0.0064.
Values may be sent and summed in bfloat16 or wider, within the bound.
No kernel may reach another device: no remote copies, remote signals or barrier semaphores. Data moves between devices by JAX's collectives and lax.ppermute only.
A program may use at most 128 MiB of HBM per device.

v0:
```python
import jax
import jax.numpy as jnp
from jax import lax
from jax.sharding import PartitionSpec as P


def expert_rows(inputs, grads_in, weight_gate, weight_up, weight_down):
    gate_pre = jnp.dot(inputs, weight_gate, preferred_element_type=jnp.float32)
    up_pre = jnp.dot(inputs, weight_up, preferred_element_type=jnp.float32)
    sigmoid_gate = jax.nn.sigmoid(gate_pre)
    activated = gate_pre * sigmoid_gate
    hidden = (activated * up_pre).astype(jnp.bfloat16)
    hidden_grad = jnp.dot(grads_in, weight_down.T, preferred_element_type=jnp.float32)
    up_grad = (hidden_grad * activated).astype(jnp.bfloat16)
    gate_grad = (
        hidden_grad * up_pre * sigmoid_gate * (1.0 + gate_pre * (1.0 - sigmoid_gate))
    ).astype(jnp.bfloat16)
    row_grad = (
        jnp.dot(gate_grad, weight_gate.T, preferred_element_type=jnp.float32)
        + jnp.dot(up_grad, weight_up.T, preferred_element_type=jnp.float32)
    ).astype(jnp.bfloat16)
    return (hidden, gate_grad, up_grad, row_grad)


def slot_numbers(expert_ids, experts):
    onehot = (expert_ids[:, None] == jnp.arange(experts, dtype=jnp.int32)[None, :]).astype(
        jnp.int32
    )
    running = jnp.cumsum(onehot, axis=0, dtype=jnp.int32)
    return (
        jnp.sum(running * onehot, axis=1, dtype=jnp.int32) - 1,
        jnp.sum(onehot, axis=0, dtype=jnp.int32),
    )


def local(tokens, out_grad, gate_probs, routes, w_gate, w_up, w_down):
    experts = lax.axis_size("expert")
    tok_count = tokens.shape[0]
    width = tokens.shape[1]
    top_count = routes.shape[1]
    capacity = tok_count * top_count * 5 // (4 * experts)
    row_total = experts * capacity
    weight_gate = w_gate[0]
    weight_up = w_up[0]
    weight_down = w_down[0]
    expert_ids = routes.reshape(-1)
    slots, counts = slot_numbers(expert_ids, experts)
    places = expert_ids * capacity + slots
    route_inputs = jnp.repeat(tokens, top_count, axis=0)
    route_grads = (
        (gate_probs[:, :, None] * out_grad[:, None, :].astype(jnp.float32))
        .astype(jnp.bfloat16)
        .reshape(-1, width)
    )
    send_inputs = (
        jnp.zeros((row_total, width), jnp.bfloat16)
        .at[places]
        .set(route_inputs)
        .reshape(experts, capacity, width)
    )
    send_grads = (
        jnp.zeros((row_total, width), jnp.bfloat16)
        .at[places]
        .set(route_grads)
        .reshape(experts, capacity, width)
    )
    got_inputs, got_grads = (
        lax.all_to_all(send_inputs, "expert", split_axis=0, concat_axis=0, tiled=True),
        lax.all_to_all(send_grads, "expert", split_axis=0, concat_axis=0, tiled=True),
    )
    flat_in = got_inputs.reshape(row_total, width)
    flat_grad = got_grads.reshape(row_total, width)
    hidden, gate_grad, up_grad, row_grad = expert_rows(
        flat_in, flat_grad, weight_gate, weight_up, weight_down
    )
    returned = lax.all_to_all(
        row_grad.reshape(experts, capacity, width),
        "expert",
        split_axis=0,
        concat_axis=0,
        tiled=True,
    )
    gate_acc = jnp.dot(flat_in.T, gate_grad, preferred_element_type=jnp.float32)
    up_acc = jnp.dot(flat_in.T, up_grad, preferred_element_type=jnp.float32)
    down_acc = jnp.dot(hidden.T, flat_grad, preferred_element_type=jnp.float32)
    gathered = returned.reshape(row_total, width)[places].reshape(tok_count, top_count, width)
    tokens_grad = jnp.sum(gathered, axis=1, dtype=jnp.float32).astype(jnp.bfloat16)
    gate_wgrad = gate_acc.astype(jnp.bfloat16)[None]
    up_wgrad = up_acc.astype(jnp.bfloat16)[None]
    down_wgrad = down_acc.astype(jnp.bfloat16)[None]
    return (tokens_grad, gate_wgrad, up_wgrad, down_wgrad)


def solution(mesh):
    return jax.shard_map(
        local,
        mesh=mesh,
        in_specs=(
            P(("groups", "expert"), None),
            P(("groups", "expert"), None),
            P(("groups", "expert"), None),
            P(("groups", "expert"), None),
            P("expert", None, None),
            P("expert", None, None),
            P("expert", None, None),
        ),
        out_specs=(
            P(("groups", "expert"), None),
            P(("groups", "expert"), None, None),
            P(("groups", "expert"), None, None),
            P(("groups", "expert"), None, None),
        ),
        check_vma=False,
    )
```

profile of v0, /device:TPU:13, one launch (start us, length us, event | category | flops | bytes accessed | tf_op | source)
XLA Modules:
  0.0 412.5 jit_solution(14100621843344244033)
XLA Ops:
  0.6 0.0 copy-start
  0.6 0.8 broadcast_multiply_fusion
  1.5 0.8 copy.14
  2.2 0.1 eq.29
  2.3 0.1 eq.25
  2.4 0.1 copy.13
  2.5 0.1 mul.60
  2.6 4.5 %reduce-window.6 = s32[16,8,128]{2,1,0:T(8,128)S(1)} reduce-window(s32[16,8,128]{2,1,0:T(8,128)S(1)} %fusion.26, s32[]{:T(128)} %constant.8.clone.1), window={size=1x1x128 pad=0_0x0_0x127_0}, to_apply=%region_0.0 | reduce-window | flops 2080768 | bytes 131076 | tf_op jit(solution)/shard_map/reduce-window
  7.2 0.1 slice.10
  7.2 0.1 copy.16
  7.4 0.1 copy.17
  7.5 0.1 broadcast_add_fusion
  7.6 10.1 %scatter_custom_fusion.1 = bf16[1280,2048]{1,0:T(8,128)(2,1)} fusion(s32[1024]{0:T(1024)S(1)} %bitcast.70, bf16[]{:T(256)} %constant.6.clone.1, bf16[128,2048]{1,0:T(8,128)(2,1)} %param.7), kind=kCustom, calls=%fused_computation.8 | custom fusion | bytes 5767170 | tf_op jit(solution)/shard_map/scatter | solution.py:58
  17.7 0.0 copy-start.7
  17.7 6.7 %all-to-all-start.1 = ((bf16[16,80,2048]{2,1,0:T(8,128)(2,1)}), bf16[16,80,2048]{2,1,0:T(8,128)(2,1)}, u32[]{:S(2)}, u32[]{:S(2)}) async-start(bf16[16,80,2048]{2,1,0:T(8,128)(2,1)} %bitcast.66), calls=%async_computation.1 | async-start | bytes 10485760 | tf_op jit(solution)/shard_map/all_to_all | solution.py:68
  24.4 0.0 copy-done.7
  24.4 0.1 copy.18
  24.5 0.1 mul.62
  24.6 0.0 copy-done.6
  24.6 0.1 convert_element_type.37
  24.7 10.1 %scatter_custom_fusion = bf16[1280,2048]{1,0:T(8,128)(2,1)} fusion(s32[1024]{0:T(1024)S(1)} %bitcast.71, f32[128,2048]{1,0:T(8,128)S(1)} %convert_element_type.37, f32[1024]{0:T(1024)S(1)} %mul.62, bf16[]{:T(256)} %constant.6.clone.1), kind=kCustom, calls=%fused_computation.6 | custom fusion | flops 4194304 | bytes 6295554 | tf_op jit(solution)/shard_map/scatter | solution.py:64
  34.8 104.5 %all-to-all-done.1 = bf16[16,80,2048]{2,1,0:T(8,128)(2,1)} async-done(((bf16[16,80,2048]{2,1,0:T(8,128)(2,1)}), bf16[16,80,2048]{2,1,0:T(8,128)(2,1)}, u32[]{:S(2)}, u32[]{:S(2)}) %all-to-all-start.1) | async-done | bytes 5242912 | tf_op jit(solution)/shard_map/all_to_all | solution.py:68
  139.3 4.9 %all-to-all-start = ((bf16[16,80,2048]{2,1,0:T(8,128)(2,1)}), bf16[16,80,2048]{2,1,0:T(8,128)(2,1)}, u32[]{:S(2)}, u32[]{:S(2)}) async-start(bf16[16,80,2048]{2,1,0:T(8,128)(2,1)} %bitcast.65), calls=%async_computation | async-start | bytes 10485760 | tf_op jit(solution)/shard_map/all_to_all | solution.py:69
  144.2 0.0 copy-done
  144.2 0.0 copy-start.1
  144.3 6.8 %fusion.16 = f32[1280,384]{1,0:T(8,128)} fusion(bf16[1280,2048]{1,0:T(8,128)(2,1)} %bitcast.10, bf16[1,2048,384]{2,1,0:T(8,128)(2,1)S(1)} %copy-done), kind=kOutput, calls=%fused_computation.28 | convolution fusion | flops 2013265920 | bytes 8781824 | tf_op jit(solution)/shard_map/dot_general | solution.py:8
  151.0 0.0 copy-done.1
  151.0 6.6 %fusion.19 = f32[1280,384]{1,0:T(8,128)} fusion(bf16[1280,2048]{1,0:T(8,128)(2,1)} %bitcast.10, bf16[1,2048,384]{2,1,0:T(8,128)(2,1)S(1)} %copy-done.1), kind=kOutput, calls=%fused_computation.31 | convolution fusion | flops 2013265920 | bytes 8781824 | tf_op jit(solution)/shard_map/dot_general | solution.py:9
  157.7 101.5 %all-to-all-done = bf16[16,80,2048]{2,1,0:T(8,128)(2,1)} async-done(((bf16[16,80,2048]{2,1,0:T(8,128)(2,1)}), bf16[16,80,2048]{2,1,0:T(8,128)(2,1)}, u32[]{:S(2)}, u32[]{:S(2)}) %all-to-all-start) | async-done | bytes 5242912 | tf_op jit(solution)/shard_map/all_to_all | solution.py:69
  259.2 7.5 %multiply_convert_fusion.1 = (bf16[1280,384]{1,0:T(8,128)(2,1)S(1)}, bf16[1280,384]{1,0:T(8,128)(2,1)S(1)}) fusion(f32[1280,384]{1,0:T(8,128)} %fusion.16, f32[1280,384]{1,0:T(8,128)} %fusion.19, bf16[1280,2048]{1,0:T(8,128)(2,1)} %bitcast.6, bf16[1,384,2048]{2,1,0:T(8,128)(2,1)} %param.13), kind=kOutput, calls=%fused_computation.22 | convolution fusion | flops 2019655680 | bytes 12713984 | tf_op jit(solution)/shard_map/dot_general | solution.py:13
  266.7 0.0 copy-start.2
  266.7 0.0 copy-start.4
  266.7 2.9 fusion.14
  269.7 0.0 copy-done.2
  269.7 0.0 copy-done.4
  269.7 4.7 %add_convert_fusion = bf16[1280,2048]{1,0:T(8,128)(2,1)} fusion(f32[1280,2048]{1,0:T(8,128)S(1)} %fusion.14, bf16[1280,384]{1,0:T(8,128)(2,1)S(1)} %get-tuple-element.4, bf16[1,2048,384]{2,1,0:T(8,128)(2,1)S(1)} %copy-done.1), kind=kOutput, calls=%fused_computation.3 | convolution fusion | flops 2018508800 | bytes 18284544 | tf_op jit(solution)/shard_map/dot_general | solution.py:20
  274.4 5.3 %all-to-all-start.2 = ((bf16[16,80,2048]{2,1,0:T(8,128)(2,1)}), bf16[16,80,2048]{2,1,0:T(8,128)(2,1)}, u32[]{:S(2)}, u32[]{:S(2)}) async-start(bf16[16,80,2048]{2,1,0:T(8,128)(2,1)} %bitcast.67), calls=%async_computation.2 | async-start | bytes 10485760 | tf_op jit(solution)/shard_map/all_to_all | solution.py:76
  279.7 0.0 copy-done.5
  279.7 0.0 copy-start.3
  279.7 6.6 %fusion.10 = bf16[1,2048,384]{2,1,0:T(8,128)(2,1)} fusion(bf16[1280,2048]{1,0:T(8,128)(2,1)} %bitcast.10, bf16[1280,384]{1,0:T(8,128)(2,1)S(1)} %copy-done.5), kind=kOutput, calls=%fused_computation.18 | convolution fusion | flops 2014052352 | bytes 7798784 | tf_op jit(solution)/shard_map/dot_general | solution.py:84
  286.4 0.0 copy-done.3
  286.4 6.7 %fusion.9 = bf16[1,2048,384]{2,1,0:T(8,128)(2,1)} fusion(bf16[1280,2048]{1,0:T(8,128)(2,1)} %bitcast.10, bf16[1280,384]{1,0:T(8,128)(2,1)S(1)} %copy-done.3), kind=kOutput, calls=%fused_computation.17 | convolution fusion | flops 2014052352 | bytes 7798784 | tf_op jit(solution)/shard_map/dot_general | solution.py:83
  293.1 0.0 copy-done.8
  293.1 0.0 copy-done.9
  293.1 6.0 %fusion.11 = bf16[1,384,2048]{2,1,0:T(8,128)(2,1)} fusion(bf16[1280,2048]{1,0:T(8,128)(2,1)} %bitcast.6, f32[1280,384]{1,0:T(8,128)S(1)} %copy-done.9, f32[1280,384]{1,0:T(8,128)S(1)} %copy-done.8), kind=kOutput, calls=%fused_computation.19 | convolution fusion | flops 2017001472 | bytes 10747904 | tf_op jit(solution)/shard_map/dot_general | solution.py:85
  299.1 95.5 %all-to-all-done.2 = bf16[16,80,2048]{2,1,0:T(8,128)(2,1)} async-done(((bf16[16,80,2048]{2,1,0:T(8,128)(2,1)}), bf16[16,80,2048]{2,1,0:T(8,128)(2,1)}, u32[]{:S(2)}, u32[]{:S(2)}) %all-to-all-start.2) | async-done | bytes 5242912 | tf_op jit(solution)/shard_map/all_to_all | solution.py:76
  394.6 12.0 %gather_fusion = bf16[1024,2048]{1,0:T(8,128)(2,1)} fusion(bf16[1280,2048]{1,0:T(8,128)(2,1)} %bitcast.14, s32[1024]{0:T(1024)S(1)} %broadcast_clamp_fusion), kind=kCustom, calls=%fused_computation | custom fusion | bytes 8392704 | tf_op jit(solution)/shard_map/gather | solution.py:86
  406.6 5.9 %bitcast_reduce_fusion = bf16[128,2048]{1,0:T(8,128)(2,1)} fusion(bf16[1024,2048]{1,0:T(8,128)(2,1)} %gather_fusion), kind=kLoop, calls=%fused_computation.7 | loop fusion | flops 1835008 | bytes 4718592 | tf_op jit(solution)/shard_map/reduce_sum | solution.py:87
  (11 shorter events, 0.1 us)
Async XLA Ops:
  0.6 143.6 %copy-start = (bf16[1,2048,384]{2,1,0:T(8,128)(2,1)S(1)}, bf16[1,2048,384]{2,1,0:T(8,128)(2,1)}, u32[]{:S(2)}) copy-start(bf16[1,2048,384]{2,1,0:T(8,128)(2,1)} %param.11) | copy-start | bytes 4718596
  17.7 6.7 %copy-start.7 = (f32[128,8]{0,1:T(8,128)S(1)}, f32[128,8]{0,1:T(8,128)}, u32[]{:S(2)}) copy-start(f32[128,8]{0,1:T(8,128)} %param.9) | copy-start | bytes 12292
  17.7 6.9 %copy-start.6 = (bf16[128,2048]{1,0:T(8,128)(2,1)S(1)}, bf16[128,2048]{1,0:T(8,128)(2,1)}, u32[]{:S(2)}) copy-start(bf16[128,2048]{1,0:T(8,128)(2,1)} %param.8) | copy-start | bytes 1572868
  17.7 121.6 %all-to-all-start.1 = ((bf16[16,80,2048]{2,1,0:T(8,128)(2,1)}), bf16[16,80,2048]{2,1,0:T(8,128)(2,1)}, u32[]{:S(2)}, u32[]{:S(2)}) async-start(bf16[16,80,2048]{2,1,0:T(8,128)(2,1)} %bitcast.66), calls=%async_computation.1 | async-start | bytes 10485760 | tf_op jit(solution)/shard_map/all_to_all | solution.py:68
  139.3 119.8 %all-to-all-start = ((bf16[16,80,2048]{2,1,0:T(8,128)(2,1)}), bf16[16,80,2048]{2,1,0:T(8,128)(2,1)}, u32[]{:S(2)}, u32[]{:S(2)}) async-start(bf16[16,80,2048]{2,1,0:T(8,128)(2,1)} %bitcast.65), calls=%async_computation | async-start | bytes 10485760 | tf_op jit(solution)/shard_map/all_to_all | solution.py:69
  144.2 6.8 %copy-start.1 = (bf16[1,2048,384]{2,1,0:T(8,128)(2,1)S(1)}, bf16[1,2048,384]{2,1,0:T(8,128)(2,1)}, u32[]{:S(2)}) copy-start(bf16[1,2048,384]{2,1,0:T(8,128)(2,1)} %param.12) | copy-start | bytes 4718596
  266.7 3.0 copy-start.2
  266.7 3.0 copy-start.4
  274.4 5.3 %copy-start.5 = (bf16[1280,384]{1,0:T(8,128)(2,1)S(1)}, bf16[1280,384]{1,0:T(8,128)(2,1)}, u32[]{:S(2)}) copy-start(bf16[1280,384]{1,0:T(8,128)(2,1)} %copy-done.4) | copy-start | bytes 2949124
  274.4 120.2 %all-to-all-start.2 = ((bf16[16,80,2048]{2,1,0:T(8,128)(2,1)}), bf16[16,80,2048]{2,1,0:T(8,128)(2,1)}, u32[]{:S(2)}, u32[]{:S(2)}) async-start(bf16[16,80,2048]{2,1,0:T(8,128)(2,1)} %bitcast.67), calls=%async_computation.2 | async-start | bytes 10485760 | tf_op jit(solution)/shard_map/all_to_all | solution.py:76
  279.7 6.7 %copy-start.3 = (bf16[1280,384]{1,0:T(8,128)(2,1)S(1)}, bf16[1280,384]{1,0:T(8,128)(2,1)}, u32[]{:S(2)}) copy-start(bf16[1280,384]{1,0:T(8,128)(2,1)} %copy-done.2) | copy-start | bytes 2949124
  286.4 6.7 %copy-start.8 = (f32[1280,384]{1,0:T(8,128)S(1)}, f32[1280,384]{1,0:T(8,128)}, u32[]{:S(2)}) copy-start(f32[1280,384]{1,0:T(8,128)} %fusion.16) | copy-start | bytes 5898244
  286.4 6.7 %copy-start.9 = (f32[1280,384]{1,0:T(8,128)S(1)}, f32[1280,384]{1,0:T(8,128)}, u32[]{:S(2)}) copy-start(f32[1280,384]{1,0:T(8,128)} %fusion.19) | copy-start | bytes 5898244
where the time goes:
time: 413 us; the launch traced here: 412 us
  waiting for transfers between devices  302 us (73%)
  matrix products  47.9 us (12%)
  local copies, waits for them, and re-layouts  23.7 us (6%)
  other arithmetic  21.6 us (5%)
  starting transfers between devices  16.9 us (4%)
    all_to_all x1, waiting for transfers between devices, local(): lax.all_to_all(send_inputs, 'expert', split_axis=0, concat_axis=0, tiled=...  105 us
    all_to_all x1, waiting for transfers between devices, local(): lax.all_to_all(send_grads, 'expert', split_axis=0, concat_axis=0, tiled=T...  102 us
    all_to_all x1, waiting for transfers between devices, local(): lax.all_to_all(row_grad.reshape(experts, capacity, width), 'expert', spli...  95.5 us
    gather x1, local copies, waits for them, and re-layouts, local(): returned.reshape(row_total, width)[places]  12 us
    scatter x1, other arithmetic, local(): send_grads = jnp.zeros((row_total, width), jnp.bfloat16).at[places].set(r...  10.1 us
    scatter x1, local copies, waits for them, and re-layouts, local(): send_inputs = jnp.zeros((row_total, width), jnp.bfloat16).at[places].set(...  10.1 us
  transfers between devices with their start and end apart: 3, of which 3 were waited for; matrix products, arithmetic and copies ran while one was open for 10% of the time, Pallas kernels for 0%

commit v1 on v0

--- a/solution.py
+++ b/solution.py
@@ -2,6 +2,22 @@
 import jax.numpy as jnp
 from jax import lax
 from jax.sharding import PartitionSpec as P
+
+
+def swapped_with_each(shard, axis, split, join):
+    ways, here = (lax.axis_size(axis), lax.axis_index(axis))
+    width = shard.shape[split] // ways
+    dims = list(shard.shape)
+    dims[split] = width
+    height = dims[join]
+    dims[join] = height * ways
+    full = jnp.zeros(dims, shard.dtype)
+    for mask in range(ways):
+        part = lax.dynamic_slice_in_dim(shard, (here ^ mask) * width, width, axis=split)
+        if mask:
+            part = lax.ppermute(part, axis, [(d, d ^ mask) for d in range(ways)])
+        full = lax.dynamic_update_slice_in_dim(full, part, (here ^ mask) * height, axis=join)
+    return full
 
 
 def expert_rows(inputs, grads_in, weight_gate, weight_up, weight_down):
@@ -66,7 +82,7 @@
     )
     got_inputs, got_grads = (
         lax.all_to_all(send_inputs, "expert", split_axis=0, concat_axis=0, tiled=True),
-        lax.all_to_all(send_grads, "expert", split_axis=0, concat_axis=0, tiled=True),
+        swapped_with_each(send_grads, "expert", 0, 0),
     )
     flat_in = got_inputs.reshape(row_total, width)
     flat_grad = got_grads.reshape(row_total, width)

time: 413 us -> 433 us (1.048); the launches traced: 412 us -> 424 us
  waiting for transfers between devices: 302 us -> 274 us
  starting transfers between devices: 16.9 us -> 42.3 us
  local copies, waits for them, and re-layouts: 23.7 us -> 41.3 us
    ppermute x0 -> x15, waiting for transfers between devices: none -> 178 us  [swapped_with_each(): part = lax.ppermute(part, axis, [(d, d ^ mask) for d in range(ways)])]
    all_to_all x1, waiting for transfers between devices: 105 us -> 0.01 us  [local(): lax.all_to_all(send_inputs, 'expert', split_axis=0, concat_axis=0, tiled=...]
    all_to_all x1 -> x0, waiting for transfers between devices: 102 us -> none  [local(): lax.all_to_all(send_grads, 'expert', split_axis=0, concat_axis=0, tiled=T...]
    ppermute x0 -> x15, starting transfers between devices: none -> 29.7 us  [swapped_with_each(): part = lax.ppermute(part, axis, [(d, d ^ mask) for d in range(ways)])]
    dynamic_update_slice x0 -> x15, local copies, waits for them, and re-layouts: none -> 11.3 us  [swapped_with_each(): lax.dynamic_update_slice_in_dim(full, part, (here ^ mask) * height, axis=...]
    all_to_all x1 -> x0, starting transfers between devices: 4.91 us -> none  [local(): lax.all_to_all(send_grads, 'expert', split_axis=0, concat_axis=0, tiled=T...]
  transfers between devices with their start and end apart: 3 -> 17, of which waited for: 3 -> 12; matrix products, arithmetic and copies ran while one was open for 10% -> 11% of each run, Pallas kernels for 0% -> 0%
where the time goes in v1:
time: 433 us; the launch traced here: 424 us
  waiting for transfers between devices  274 us (63%)
  matrix products  44.2 us (10%)
  starting transfers between devices  42.3 us (10%)
  local copies, waits for them, and re-layouts  41.3 us (10%)
  other arithmetic  22 us (5%)
    ppermute x15, waiting for transfers between devices, swapped_with_each(): part = lax.ppermute(part, axis, [(d, d ^ mask) for d in range(ways)])  178 us
    all_to_all x1, waiting for transfers between devices, local(): lax.all_to_all(row_grad.reshape(experts, capacity, width), 'expert', spli...  95.5 us
    ppermute x15, starting transfers between devices, swapped_with_each(): part = lax.ppermute(part, axis, [(d, d ^ mask) for d in range(ways)])  29.7 us
    gather x1, local copies, waits for them, and re-layouts, local(): returned.reshape(row_total, width)[places]  12.3 us
    dynamic_update_slice x15, local copies, waits for them, and re-layouts, swapped_with_each(): lax.dynamic_update_slice_in_dim(full, part, (here ^ mask) * height, axis=...  11.3 us
    scatter x1, other arithmetic, local(): send_grads = jnp.zeros((row_total, width), jnp.bfloat16).at[places].set(r...  10.5 us
    scatter x1, local copies, waits for them, and re-layouts, local(): send_inputs = jnp.zeros((row_total, width), jnp.bfloat16).at[places].set(...  10.1 us
  transfers between devices with their start and end apart: 17, of which 12 were waited for; matrix products, arithmetic and copies ran while one was open for 11% of the time, Pallas kernels for 0%

profile of v1, /device:TPU:13, one launch (start us, length us, event | category | flops | bytes accessed | tf_op | source)
XLA Modules:
  0.0 424.4 jit_solution(1696626243027350214)
XLA Ops:
  0.6 0.8 broadcast_multiply_fusion
  1.5 0.8 copy.14
  2.6 4.5 %reduce-window.6 = s32[16,8,128]{2,1,0:T(8,128)S(1)} reduce-window(s32[16,8,128]{2,1,0:T(8,128)S(1)} %fusion.26, s32[]{:T(128)} %constant.25.clone.1), window={size=1x1x128 pad=0_0x0_0x127_0}, to_apply=%region_0.0 | reduce-window | flops 2080768 | bytes 131076 | tf_op jit(solution)/shard_map/reduce-window
  7.6 10.1 %scatter_custom_fusion.1 = bf16[1280,2048]{1,0:T(8,128)(2,1)} fusion(s32[1024]{0:T(1024)S(1)} %bitcast.70, bf16[]{:T(256)} %constant.23.clone.1, bf16[128,2048]{1,0:T(8,128)(2,1)} %param.7), kind=kCustom, calls=%fused_computation.8 | custom fusion | bytes 5767170 | tf_op jit(solution)/shard_map/scatter | solution.py:74
  17.7 6.7 %all-to-all-start = ((bf16[16,80,2048]{2,1,0:T(8,128)(2,1)}), bf16[16,80,2048]{2,1,0:T(8,128)(2,1)}, u32[]{:S(2)}, u32[]{:S(2)}) async-start(bf16[16,80,2048]{2,1,0:T(8,128)(2,1)} %bitcast.65), calls=%async_computation | async-start | bytes 10485760 | tf_op jit(solution)/shard_map/all_to_all | solution.py:84
  24.8 10.5 %scatter_custom_fusion = bf16[1280,2048]{1,0:T(8,128)(2,1)} fusion(s32[1024]{0:T(1024)S(1)} %bitcast.71, f32[128,2048]{1,0:T(8,128)S(1)} %convert_element_type.37, f32[1024]{0:T(1024)S(1)} %mul.62, bf16[]{:T(256)} %constant.23.clone.1), kind=kCustom, calls=%fused_computation.6 | custom fusion | flops 4194304 | bytes 6295554 | tf_op jit(solution)/shard_map/scatter | solution.py:80
  35.4 3.3 broadcast_in_dim.10
  38.7 1.0 copy-done.2
  39.7 1.6 constant_dynamic-slice_fusion.14
  41.9 2.4 collective-permute-start.14
  44.6 1.4 collective-permute-start.12
  46.1 1.2 collective-permute-start.2
  47.3 0.8 constant_dynamic-update-slice_fusion.13
  48.1 12.7 %collective-permute-done.1 = bf16[1,80,2048]{2,1,0:T(8,128)(2,1)S(1)} collective-permute-done((bf16[1,80,2048]{2,1,0:T(8,128)(2,1)S(1)}, bf16[1,80,2048]{2,1,0:T(8,128)(2,1)S(1)}, u32[]{:S(2)}, u32[]{:S(2)}) %collective-permute-start.1) | collective-permute-done | bytes 327712 | tf_op jit(solution)/shard_map/ppermute | solution.py:18
  62.0 6.0 %collective-permute-done.2 = bf16[1,80,2048]{2,1,0:T(8,128)(2,1)S(1)} collective-permute-done((bf16[1,80,2048]{2,1,0:T(8,128)(2,1)S(1)}, bf16[1,80,2048]{2,1,0:T(8,128)(2,1)S(1)}, u32[]{:S(2)}, u32[]{:S(2)}) %collective-permute-start.2) | collective-permute-done | bytes 327712 | tf_op jit(solution)/shard_map/ppermute | solution.py:18
  68.0 8.8 %collective-permute-start.4 = (bf16[1,80,2048]{2,1,0:T(8,128)(2,1)S(1)}, bf16[1,80,2048]{2,1,0:T(8,128)(2,1)S(1)}, u32[]{:S(2)}, u32[]{:S(2)}) collective-permute-start(bf16[1,80,2048]{2,1,0:T(8,128)(2,1)S(1)} %get-tuple-element.14), channel_id=1, source_target_pairs={{0,5},{1,4},{2,7},{3,6},{4,1},{5,0},{6,3},{7,2},{8,13},{9,12},{10,... | collective-permute-start | bytes 983048 | tf_op jit(solution)/shard_map/ppermute | solution.py:18
  76.8 0.7 constant_dynamic-update-slice_fusion.11
  77.6 61.7 %collective-permute-done.3 = bf16[1,80,2048]{2,1,0:T(8,128)(2,1)S(1)} collective-permute-done((bf16[1,80,2048]{2,1,0:T(8,128)(2,1)S(1)}, bf16[1,80,2048]{2,1,0:T(8,128)(2,1)S(1)}, u32[]{:S(2)}, u32[]{:S(2)}) %collective-permute-start.3) | collective-permute-done | bytes 327712 | tf_op jit(solution)/shard_map/ppermute | solution.py:18
  139.3 0.8 constant_dynamic-update-slice_fusion.10
  140.0 7.2 %collective-permute-done.4 = bf16[1,80,2048]{2,1,0:T(8,128)(2,1)S(1)} collective-permute-done((bf16[1,80,2048]{2,1,0:T(8,128)(2,1)S(1)}, bf16[1,80,2048]{2,1,0:T(8,128)(2,1)S(1)}, u32[]{:S(2)}, u32[]{:S(2)}) %collective-permute-start.4) | collective-permute-done | bytes 327712 | tf_op jit(solution)/shard_map/ppermute | solution.py:18
  147.2 0.8 constant_dynamic-update-slice_fusion.9
  148.0 4.5 %collective-permute-done.5 = bf16[1,80,2048]{2,1,0:T(8,128)(2,1)S(1)} collective-permute-done((bf16[1,80,2048]{2,1,0:T(8,128)(2,1)S(1)}, bf16[1,80,2048]{2,1,0:T(8,128)(2,1)S(1)}, u32[]{:S(2)}, u32[]{:S(2)}) %collective-permute-start.5) | collective-permute-done | bytes 327712 | tf_op jit(solution)/shard_map/ppermute | solution.py:18
  152.5 9.6 %collective-permute-start.7 = (bf16[1,80,2048]{2,1,0:T(8,128)(2,1)S(1)}, bf16[1,80,2048]{2,1,0:T(8,128)(2,1)S(1)}, u32[]{:S(2)}, u32[]{:S(2)}) collective-permute-start(bf16[1,80,2048]{2,1,0:T(8,128)(2,1)S(1)} %get-tuple-element.11), channel_id=1, source_target_pairs={{0,8},{1,9},{2,10},{3,11},{4,12},{5,13},{6,14},{7,15},{8,0},{9,1},... | collective-permute-start | bytes 983048 | tf_op jit(solution)/shard_map/ppermute | solution.py:18
  162.9 2.2 collective-permute-done.6
  165.0 4.5 %collective-permute-start.8 = (bf16[1,80,2048]{2,1,0:T(8,128)(2,1)S(1)}, bf16[1,80,2048]{2,1,0:T(8,128)(2,1)S(1)}, u32[]{:S(2)}, u32[]{:S(2)}) collective-permute-start(bf16[1,80,2048]{2,1,0:T(8,128)(2,1)S(1)} %get-tuple-element.10), channel_id=1, source_target_pairs={{0,9},{1,8},{2,11},{3,10},{4,13},{5,12},{6,15},{7,14},{8,1},{9,0},... | collective-permute-start | bytes 983048 | tf_op jit(solution)/shard_map/ppermute | solution.py:18
  169.5 0.7 constant_dynamic-update-slice_fusion.7
  170.3 36.7 %collective-permute-done.7 = bf16[1,80,2048]{2,1,0:T(8,128)(2,1)S(1)} collective-permute-done((bf16[1,80,2048]{2,1,0:T(8,128)(2,1)S(1)}, bf16[1,80,2048]{2,1,0:T(8,128)(2,1)S(1)}, u32[]{:S(2)}, u32[]{:S(2)}) %collective-permute-start.7) | collective-permute-done | bytes 327712 | tf_op jit(solution)/shard_map/ppermute | solution.py:18
  207.8 13.3 %collective-permute-done.8 = bf16[1,80,2048]{2,1,0:T(8,128)(2,1)S(1)} collective-permute-done((bf16[1,80,2048]{2,1,0:T(8,128)(2,1)S(1)}, bf16[1,80,2048]{2,1,0:T(8,128)(2,1)S(1)}, u32[]{:S(2)}, u32[]{:S(2)}) %collective-permute-start.8) | collective-permute-done | bytes 327712 | tf_op jit(solution)/shard_map/ppermute | solution.py:18
  221.1 0.8 constant_dynamic-update-slice_fusion.5
  221.8 13.3 %collective-permute-done.9 = bf16[1,80,2048]{2,1,0:T(8,128)(2,1)S(1)} collective-permute-done((bf16[1,80,2048]{2,1,0:T(8,128)(2,1)S(1)}, bf16[1,80,2048]{2,1,0:T(8,128)(2,1)S(1)}, u32[]{:S(2)}, u32[]{:S(2)}) %collective-permute-start.9) | collective-permute-done | bytes 327712 | tf_op jit(solution)/shard_map/ppermute | solution.py:18
  235.4 0.8 constant_dynamic-update-slice_fusion.4
  236.2 13.0 %collective-permute-done.10 = bf16[1,80,2048]{2,1,0:T(8,128)(2,1)S(1)} collective-permute-done((bf16[1,80,2048]{2,1,0:T(8,128)(2,1)S(1)}, bf16[1,80,2048]{2,1,0:T(8,128)(2,1)S(1)}, u32[]{:S(2)}, u32[]{:S(2)}) %collective-permute-start.10) | collective-permute-done | bytes 327712 | tf_op jit(solution)/shard_map/ppermute | solution.py:18
  249.9 7.3 %collective-permute-done.11 = bf16[1,80,2048]{2,1,0:T(8,128)(2,1)S(1)} collective-permute-done((bf16[1,80,2048]{2,1,0:T(8,128)(2,1)S(1)}, bf16[1,80,2048]{2,1,0:T(8,128)(2,1)S(1)}, u32[]{:S(2)}, u32[]{:S(2)}) %collective-permute-start.11) | collective-permute-done | bytes 327712 | tf_op jit(solution)/shard_map/ppermute | solution.py:18
  257.2 0.8 constant_dynamic-update-slice_fusion.2
  258.7 0.7 constant_dynamic-update-slice_fusion
  259.5 0.7 constant_dynamic-update-slice_fusion.14
  260.2 4.9 %fusion.16 = f32[1280,384]{1,0:T(8,128)S(1)} fusion(bf16[1280,2048]{1,0:T(8,128)(2,1)} %bitcast.10, bf16[1,2048,384]{2,1,0:T(8,128)(2,1)S(1)} %copy-done), kind=kOutput, calls=%fused_computation.28 | convolution fusion | flops 2013265920 | bytes 8781824 | tf_op jit(solution)/shard_map/dot_general | solution.py:24
  265.2 5.6 %fusion.19 = f32[1280,384]{1,0:T(8,128)S(1)} fusion(bf16[1280,2048]{1,0:T(8,128)(2,1)} %bitcast.10, bf16[1,2048,384]{2,1,0:T(8,128)(2,1)S(1)} %copy-done.3), kind=kOutput, calls=%fused_computation.31 | convolution fusion | flops 2013265920 | bytes 8781824 | tf_op jit(solution)/shard_map/dot_general | solution.py:25
  270.8 6.8 %multiply_convert_fusion.1 = (bf16[1280,384]{1,0:T(8,128)(2,1)S(1)}, bf16[1280,384]{1,0:T(8,128)(2,1)S(1)}) fusion(f32[1280,384]{1,0:T(8,128)S(1)} %fusion.16, f32[1280,384]{1,0:T(8,128)S(1)} %fusion.19, bf16[1280,2048]{1,0:T(8,128)(2,1)} %bitcast.6, bf16[1,384,2048]{2,1,0:T(8,128)(2,1)S(1)} %copy-done.6), kind=kOutput, calls=%fused_computation.22 | convolution fusion | flops 2019655680 | bytes 12713984 | tf_op jit(solution)/shard_map/dot_general | solution.py:29
  277.6 2.9 fusion.14
  280.5 4.8 %add_convert_fusion = bf16[1280,2048]{1,0:T(8,128)(2,1)} fusion(f32[1280,2048]{1,0:T(8,128)S(1)} %fusion.14, bf16[1280,384]{1,0:T(8,128)(2,1)S(1)} %get-tuple-element.20, bf16[1,2048,384]{2,1,0:T(8,128)(2,1)S(1)} %copy-done.3), kind=kOutput, calls=%fused_computation.3 | convolution fusion | flops 2018508800 | bytes 18284544 | tf_op jit(solution)/shard_map/dot_general | solution.py:36
  285.3 5.9 %all-to-all-start.1 = ((bf16[16,80,2048]{2,1,0:T(8,128)(2,1)}), bf16[16,80,2048]{2,1,0:T(8,128)(2,1)}, u32[]{:S(2)}, u32[]{:S(2)}) async-start(bf16[16,80,2048]{2,1,0:T(8,128)(2,1)} %bitcast.67), calls=%async_computation.1 | async-start | bytes 10485760 | tf_op jit(solution)/shard_map/all_to_all | solution.py:92
  291.2 6.6 %fusion.10 = bf16[1,2048,384]{2,1,0:T(8,128)(2,1)} fusion(bf16[1280,2048]{1,0:T(8,128)(2,1)} %bitcast.10, bf16[1280,384]{1,0:T(8,128)(2,1)S(1)} %get-tuple-element.20), kind=kOutput, calls=%fused_computation.18 | convolution fusion | flops 2014052352 | bytes 7798784 | tf_op jit(solution)/shard_map/dot_general | solution.py:100
  297.8 6.7 %fusion.9 = bf16[1,2048,384]{2,1,0:T(8,128)(2,1)} fusion(bf16[1280,2048]{1,0:T(8,128)(2,1)} %bitcast.10, bf16[1280,384]{1,0:T(8,128)(2,1)S(1)} %get-tuple-element.21), kind=kOutput, calls=%fused_computation.17 | convolution fusion | flops 2014052352 | bytes 7798784 | tf_op jit(solution)/shard_map/dot_general | solution.py:99
  304.5 6.0 %fusion.11 = bf16[1,384,2048]{2,1,0:T(8,128)(2,1)} fusion(bf16[1280,2048]{1,0:T(8,128)(2,1)} %bitcast.6, f32[1280,384]{1,0:T(8,128)S(1)} %copy-done.10, f32[1280,384]{1,0:T(8,128)S(1)} %copy-done.8), kind=kOutput, calls=%fused_computation.19 | convolution fusion | flops 2017001472 | bytes 10747904 | tf_op jit(solution)/shard_map/dot_general | solution.py:101
  310.5 95.5 %all-to-all-done.1 = bf16[16,80,2048]{2,1,0:T(8,128)(2,1)} async-done(((bf16[16,80,2048]{2,1,0:T(8,128)(2,1)}), bf16[16,80,2048]{2,1,0:T(8,128)(2,1)}, u32[]{:S(2)}, u32[]{:S(2)}) %all-to-all-start.1) | async-done | bytes 5242912 | tf_op jit(solution)/shard_map/all_to_all | solution.py:92
  406.0 12.3 %gather_fusion = bf16[1024,2048]{1,0:T(8,128)(2,1)} fusion(bf16[1280,2048]{1,0:T(8,128)(2,1)} %bitcast.14, s32[1024]{0:T(1024)S(1)} %broadcast_clamp_fusion), kind=kCustom, calls=%fused_computation | custom fusion | bytes 8392704 | tf_op jit(solution)/shard_map/gather | solution.py:102
  418.3 5.9 %bitcast_reduce_fusion = bf16[128,2048]{1,0:T(8,128)(2,1)} fusion(bf16[1024,2048]{1,0:T(8,128)(2,1)} %gather_fusion), kind=kLoop, calls=%fused_computation.7 | loop fusion | flops 1835008 | bytes 4718592 | tf_op jit(solution)/shard_map/reduce_sum | solution.py:103
  (58 shorter events, 6.5 us)
Async XLA Ops:
  0.6 259.6 %copy-start = (bf16[1,2048,384]{2,1,0:T(8,128)(2,1)S(1)}, bf16[1,2048,384]{2,1,0:T(8,128)(2,1)}, u32[]{:S(2)}) copy-start(bf16[1,2048,384]{2,1,0:T(8,128)(2,1)} %param.11) | copy-start | bytes 4718596
  17.7 6.7 %copy-start.5 = (f32[128,8]{0,1:T(8,128)S(1)}, f32[128,8]{0,1:T(8,128)}, u32[]{:S(2)}) copy-start(f32[128,8]{0,1:T(8,128)} %param.9) | copy-start | bytes 12292
  17.7 6.9 %copy-start.4 = (bf16[128,2048]{1,0:T(8,128)(2,1)S(1)}, bf16[128,2048]{1,0:T(8,128)(2,1)}, u32[]{:S(2)}) copy-start(bf16[128,2048]{1,0:T(8,128)(2,1)} %param.8) | copy-start | bytes 1572868
  17.7 242.5 %all-to-all-start = ((bf16[16,80,2048]{2,1,0:T(8,128)(2,1)}), bf16[16,80,2048]{2,1,0:T(8,128)(2,1)}, u32[]{:S(2)}, u32[]{:S(2)}) async-start(bf16[16,80,2048]{2,1,0:T(8,128)(2,1)} %bitcast.65), calls=%async_computation | async-start | bytes 10485760 | tf_op jit(solution)/shard_map/all_to_all | solution.py:84
  35.4 4.4 %copy-start.2 = (bf16[1280,2048]{1,0:T(8,128)(2,1)S(1)}, bf16[1280,2048]{1,0:T(8,128)(2,1)}, u32[]{:S(2)}) copy-start(bf16[1280,2048]{1,0:T(8,128)(2,1)} %scatter_custom_fusion) | copy-start | bytes 15728644
  41.3 4.8 %collective-permute-start = (bf16[1,80,2048]{2,1,0:T(8,128)(2,1)S(1)}, bf16[1,80,2048]{2,1,0:T(8,128)(2,1)S(1)}, u32[]{:S(2)}, u32[]{:S(2)}) collective-permute-start(bf16[1,80,2048]{2,1,0:T(8,128)(2,1)S(1)} %get-tuple-element.18), channel_id=1, source_target_pairs={{0,1},{1,0},{2,3},{3,2},{4,5},{5,4},{6,7},{7,6},{8,9},{9,8},{10,11... | collective-permute-start | bytes 983048 | tf_op jit(solution)/shard_map/ppermute | solution.py:18
  41.7 19.1 %collective-permute-start.1 = (bf16[1,80,2048]{2,1,0:T(8,128)(2,1)S(1)}, bf16[1,80,2048]{2,1,0:T(8,128)(2,1)S(1)}, u32[]{:S(2)}, u32[]{:S(2)}) collective-permute-start(bf16[1,80,2048]{2,1,0:T(8,128)(2,1)S(1)} %get-tuple-element.17), channel_id=1, source_target_pairs={{0,2},{1,3},{2,0},{3,1},{4,6},{5,7},{6,4},{7,5},{8,10},{9,11},{10,... | collective-permute-start | bytes 983048 | tf_op jit(solution)/shard_map/ppermute | solution.py:18
  41.9 217.5 %collective-permute-start.14 = (bf16[1,80,2048]{2,1,0:T(8,128)(2,1)S(1)}, bf16[1,80,2048]{2,1,0:T(8,128)(2,1)S(1)}, u32[]{:S(2)}, u32[]{:S(2)}) collective-permute-start(bf16[1,80,2048]{2,1,0:T(8,128)(2,1)S(1)} %get-tuple-element.4), channel_id=1, source_target_pairs={{0,15},{1,14},{2,13},{3,12},{4,11},{5,10},{6,9},{7,8},{8,7},{9,6},... | collective-permute-start | bytes 983048 | tf_op jit(solution)/shard_map/ppermute | solution.py:18
  44.4 214.4 %collective-permute-start.13 = (bf16[1,80,2048]{2,1,0:T(8,128)(2,1)S(1)}, bf16[1,80,2048]{2,1,0:T(8,128)(2,1)S(1)}, u32[]{:S(2)}, u32[]{:S(2)}) collective-permute-start(bf16[1,80,2048]{2,1,0:T(8,128)(2,1)S(1)} %get-tuple-element.5), channel_id=1, source_target_pairs={{0,14},{1,15},{2,12},{3,13},{4,10},{5,11},{6,8},{7,9},{8,6},{9,7},... | collective-permute-start | bytes 983048 | tf_op jit(solution)/shard_map/ppermute | solution.py:18
  44.6 213.4 %collective-permute-start.12 = (bf16[1,80,2048]{2,1,0:T(8,128)(2,1)S(1)}, bf16[1,80,2048]{2,1,0:T(8,128)(2,1)S(1)}, u32[]{:S(2)}, u32[]{:S(2)}) collective-permute-start(bf16[1,80,2048]{2,1,0:T(8,128)(2,1)S(1)} %get-tuple-element.6), channel_id=1, source_target_pairs={{0,13},{1,12},{2,15},{3,14},{4,9},{5,8},{6,11},{7,10},{8,5},{9,4},... | collective-permute-start | bytes 983048 | tf_op jit(solution)/shard_map/ppermute | solution.py:18
  46.1 21.9 %collective-permute-start.2 = (bf16[1,80,2048]{2,1,0:T(8,128)(2,1)S(1)}, bf16[1,80,2048]{2,1,0:T(8,128)(2,1)S(1)}, u32[]{:S(2)}, u32[]{:S(2)}) collective-permute-start(bf16[1,80,2048]{2,1,0:T(8,128)(2,1)S(1)} %get-tuple-element.16), channel_id=1, source_target_pairs={{0,3},{1,2},{2,1},{3,0},{4,7},{5,6},{6,5},{7,4},{8,11},{9,10},{10,... | collective-permute-start | bytes 983048 | tf_op jit(solution)/shard_map/ppermute | solution.py:18
  60.8 78.5 %collective-permute-start.3 = (bf16[1,80,2048]{2,1,0:T(8,128)(2,1)S(1)}, bf16[1,80,2048]{2,1,0:T(8,128)(2,1)S(1)}, u32[]{:S(2)}, u32[]{:S(2)}) collective-permute-start(bf16[1,80,2048]{2,1,0:T(8,128)(2,1)S(1)} %get-tuple-element.15), channel_id=1, source_target_pairs={{0,4},{1,5},{2,6},{3,7},{4,0},{5,1},{6,2},{7,3},{8,12},{9,13},{10,... | collective-permute-start | bytes 983048 | tf_op jit(solution)/shard_map/ppermute | solution.py:18
  68.0 79.2 %collective-permute-start.4 = (bf16[1,80,2048]{2,1,0:T(8,128)(2,1)S(1)}, bf16[1,80,2048]{2,1,0:T(8,128)(2,1)S(1)}, u32[]{:S(2)}, u32[]{:S(2)}) collective-permute-start(bf16[1,80,2048]{2,1,0:T(8,128)(2,1)S(1)} %get-tuple-element.14), channel_id=1, source_target_pairs={{0,5},{1,4},{2,7},{3,6},{4,1},{5,0},{6,3},{7,2},{8,13},{9,12},{10,... | collective-permute-start | bytes 983048 | tf_op jit(solution)/shard_map/ppermute | solution.py:18
  139.3 13.3 %collective-permute-start.5 = (bf16[1,80,2048]{2,1,0:T(8,128)(2,1)S(1)}, bf16[1,80,2048]{2,1,0:T(8,128)(2,1)S(1)}, u32[]{:S(2)}, u32[]{:S(2)}) collective-permute-start(bf16[1,80,2048]{2,1,0:T(8,128)(2,1)S(1)} %get-tuple-element.13), channel_id=1, source_target_pairs={{0,6},{1,7},{2,4},{3,5},{4,2},{5,3},{6,0},{7,1},{8,14},{9,15},{10,... | collective-permute-start | bytes 983048 | tf_op jit(solution)/shard_map/ppermute | solution.py:18
  147.2 17.8 %collective-permute-start.6 = (bf16[1,80,2048]{2,1,0:T(8,128)(2,1)S(1)}, bf16[1,80,2048]{2,1,0:T(8,128)(2,1)S(1)}, u32[]{:S(2)}, u32[]{:S(2)}) collective-permute-start(bf16[1,80,2048]{2,1,0:T(8,128)(2,1)S(1)} %get-tuple-element.12), channel_id=1, source_target_pairs={{0,7},{1,6},{2,5},{3,4},{4,3},{5,2},{6,1},{7,0},{8,15},{9,14},{10,... | collective-permute-start | bytes 983048 | tf_op jit(solution)/shard_map/ppermute | solution.py:18
  152.5 54.5 %collective-permute-start.7 = (bf16[1,80,2048]{2,1,0:T(8,128)(2,1)S(1)}, bf16[1,80,2048]{2,1,0:T(8,128)(2,1)S(1)}, u32[]{:S(2)}, u32[]{:S(2)}) collective-permute-start(bf16[1,80,2048]{2,1,0:T(8,128)(2,1)S(1)} %get-tuple-element.11), channel_id=1, source_target_pairs={{0,8},{1,9},{2,10},{3,11},{4,12},{5,13},{6,14},{7,15},{8,0},{9,1},... | collective-permute-start | bytes 983048 | tf_op jit(solution)/shard_map/ppermute | solution.py:18
  165.0 56.0 %collective-permute-start.8 = (bf16[1,80,2048]{2,1,0:T(8,128)(2,1)S(1)}, bf16[1,80,2048]{2,1,0:T(8,128)(2,1)S(1)}, u32[]{:S(2)}, u32[]{:S(2)}) collective-permute-start(bf16[1,80,2048]{2,1,0:T(8,128)(2,1)S(1)} %get-tuple-element.10), channel_id=1, source_target_pairs={{0,9},{1,8},{2,11},{3,10},{4,13},{5,12},{6,15},{7,14},{8,1},{9,0},... | collective-permute-start | bytes 983048 | tf_op jit(solution)/shard_map/ppermute | solution.py:18
  207.0 28.1 %collective-permute-start.9 = (bf16[1,80,2048]{2,1,0:T(8,128)(2,1)S(1)}, bf16[1,80,2048]{2,1,0:T(8,128)(2,1)S(1)}, u32[]{:S(2)}, u32[]{:S(2)}) collective-permute-start(bf16[1,80,2048]{2,1,0:T(8,128)(2,1)S(1)} %get-tuple-element.9), channel_id=1, source_target_pairs={{0,10},{1,11},{2,8},{3,9},{4,14},{5,15},{6,12},{7,13},{8,2},{9,3},... | collective-permute-start | bytes 983048 | tf_op jit(solution)/shard_map/ppermute | solution.py:18
  221.1 28.1 %collective-permute-start.10 = (bf16[1,80,2048]{2,1,0:T(8,128)(2,1)S(1)}, bf16[1,80,2048]{2,1,0:T(8,128)(2,1)S(1)}, u32[]{:S(2)}, u32[]{:S(2)}) collective-permute-start(bf16[1,80,2048]{2,1,0:T(8,128)(2,1)S(1)} %get-tuple-element.8), channel_id=1, source_target_pairs={{0,11},{1,10},{2,9},{3,8},{4,15},{5,14},{6,13},{7,12},{8,3},{9,2},... | collective-permute-start | bytes 983048 | tf_op jit(solution)/shard_map/ppermute | solution.py:18
  235.1 22.1 %collective-permute-start.11 = (bf16[1,80,2048]{2,1,0:T(8,128)(2,1)S(1)}, bf16[1,80,2048]{2,1,0:T(8,128)(2,1)S(1)}, u32[]{:S(2)}, u32[]{:S(2)}) collective-permute-start(bf16[1,80,2048]{2,1,0:T(8,128)(2,1)S(1)} %get-tuple-element.7), channel_id=1, source_target_pairs={{0,12},{1,13},{2,14},{3,15},{4,8},{5,9},{6,10},{7,11},{8,4},{9,5},... | collective-permute-start | bytes 983048 | tf_op jit(solution)/shard_map/ppermute | solution.py:18
  260.2 4.9 %copy-start.3 = (bf16[1,2048,384]{2,1,0:T(8,128)(2,1)S(1)}, bf16[1,2048,384]{2,1,0:T(8,128)(2,1)}, u32[]{:S(2)}) copy-start(bf16[1,2048,384]{2,1,0:T(8,128)(2,1)} %param.12) | copy-start | bytes 4718596
  265.2 5.6 %copy-start.7 = (f32[1280,384]{1,0:T(8,128)}, f32[1280,384]{1,0:T(8,128)S(1)}, u32[]{:S(2)}) copy-start(f32[1280,384]{1,0:T(8,128)S(1)} %fusion.16) | copy-start | bytes 5898244
  265.2 5.6 %copy-start.6 = (bf16[1,384,2048]{2,1,0:T(8,128)(2,1)S(1)}, bf16[1,384,2048]{2,1,0:T(8,128)(2,1)}, u32[]{:S(2)}) copy-start(bf16[1,384,2048]{2,1,0:T(8,128)(2,1)} %param.13) | copy-start | bytes 4718596
  270.8 6.8 %copy-start.9 = (f32[1280,384]{1,0:T(8,128)}, f32[1280,384]{1,0:T(8,128)S(1)}, u32[]{:S(2)}) copy-start(f32[1280,384]{1,0:T(8,128)S(1)} %fusion.19) | copy-start | bytes 5898244
  285.3 120.7 %all-to-all-start.1 = ((bf16[16,80,2048]{2,1,0:T(8,128)(2,1)}), bf16[16,80,2048]{2,1,0:T(8,128)(2,1)}, u32[]{:S(2)}, u32[]{:S(2)}) async-start(bf16[16,80,2048]{2,1,0:T(8,128)(2,1)} %bitcast.67), calls=%async_computation.1 | async-start | bytes 10485760 | tf_op jit(solution)/shard_map/all_to_all | solution.py:92
  297.8 6.7 %copy-start.8 = (f32[1280,384]{1,0:T(8,128)S(1)}, f32[1280,384]{1,0:T(8,128)}, u32[]{:S(2)}) copy-start(f32[1280,384]{1,0:T(8,128)} %copy-done.7) | copy-start | bytes 5898244
  297.8 6.7 %copy-start.10 = (f32[1280,384]{1,0:T(8,128)S(1)}, f32[1280,384]{1,0:T(8,128)}, u32[]{:S(2)}) copy-start(f32[1280,384]{1,0:T(8,128)} %copy-done.9) | copy-start | bytes 5898244
  406.0 18.2 %copy-start.1 = (bf16[1,2048,384]{2,1,0:T(8,128)(2,1)S(1)}, bf16[1,2048,384]{2,1,0:T(8,128)(2,1)}, u32[]{:S(2)}) copy-start(bf16[1,2048,384]{2,1,0:T(8,128)(2,1)} %param.11) | copy-start | bytes 4718596
